TPU v7x, 32 devices: a whole 2x2x4 slice. The times are simulated.
32 devices in a mesh: group: 8 (over z, x), ctx: 2 (over y), wshard: 2 (over core).
Axes of the slice: x: 2, y: 2, z: 4, core: 2. Of those that a mesh axis runs over, the one named last changes fastest.
Arguments:
- inputs: bfloat16 [8192, 1536], P(('group', 'ctx', 'wshard')), may hold values from -6 to 6
- out_grad: bfloat16 [8192, 1536], P(('group', 'ctx', 'wshard')), may hold values from -6 to 6
- lengths: int32 [8, 4], P('group'), may hold values from 1 to 512, 1024 in all within a row
- permutation: int32 [8, 1024], P('group'), may hold values from 0 to 1023, each once within a row
- gain_attention: float32 [1536], replicated, may hold values from 0.5 to 1.5
- query_weight: bfloat16 [1536, 768], P('wshard'), may hold values from -0.0546875 to 0.0546875
- key_weight: bfloat16 [1536, 768], P('wshard'), may hold values from -0.0546875 to 0.0546875
- value_weight: bfloat16 [1536, 768], P('wshard'), may hold values from -0.15625 to 0.15625
- out_weight: bfloat16 [768, 1536], P('wshard'), may hold values from -3.5 to 3.5
- bucket_bias: float32 [32, 12], replicated, may hold values from -4 to 4
- gain_feedforward: float32 [1536], replicated, may hold values from 0.5 to 1.5
- gate_weight: bfloat16 [1536, 3968], P('wshard'), may hold values from -0.15625 to 0.15625
- up_weight: bfloat16 [1536, 3968], P('wshard'), may hold values from -0.15625 to 0.15625
- down_weight: bfloat16 [3968, 1536], P('wshard'), may hold values from -0.09375 to 0.09375
Outputs:
- outputs: bfloat16 [8192, 1536], P(('group', 'ctx', 'wshard'))
- input_grad: bfloat16 [8192, 1536], P(('group', 'ctx', 'wshard'))
- grad_gain_attention: float32 [1536], P(('ctx', 'wshard'))
- grad_query: float32 [1536, 768], P(('ctx', 'wshard'))
- grad_key: float32 [1536, 768], P(('ctx', 'wshard'))
- grad_value: float32 [1536, 768], P(('ctx', 'wshard'))
- grad_out: float32 [768, 1536], P(('ctx', 'wshard'))
- grad_bias: float32 [32, 12], replicated
- grad_gain_feedforward: float32 [1536], P(('ctx', 'wshard'))
- grad_gate: float32 [1536, 3968], P(('ctx', 'wshard'))
- grad_up: float32 [1536, 3968], P(('ctx', 'wshard'))
- grad_down: float32 [3968, 1536], P(None, ('ctx', 'wshard'))
Inputs may be any that keep to these rules, and one draw needn't show every extreme that they name: `lengths`: each row sums to 1024; the largest entry is 512. `permutation`: each row holds every place of its group once.
All inputs are finite; a program needn't handle non-finite values.
Results may differ from a plain program's by a relative error of at most 0.02.
Values may be sent and summed in bfloat16 or wider, within the bound.
No kernel may reach another device: no remote copies, remote signals or barrier semaphores. Data moves between devices by JAX's collectives and lax.ppermute only.
A program may use at most 320 MiB of HBM per device.

v0:
```python
import jax
import jax.numpy as jnp
from jax import lax
from jax.sharding import PartitionSpec as P

epsilon = 1e-06
highest = lax.Precision.HIGHEST
thresholds = (12, 16, 23, 32, 46, 64, 91)
masked_out = -1e30


def bucket_of(offset):
    distance = jnp.abs(offset)
    beyond = 8 + sum(((distance >= border).astype(jnp.int32) for border in thresholds))
    near_far = jnp.where(distance < 8, distance, beyond)
    return jnp.where(offset > 0, 16, 0) + near_far


def rms_norm(values, gain_vector):
    return (
        values
        * lax.rsqrt(jnp.mean(values * values, axis=-1, keepdims=True) + epsilon)
        * gain_vector
    )


def forward_product(left_side, right_side):
    return jnp.dot(left_side, right_side, preferred_element_type=jnp.float32)


def backward_product(left_side, right_side):
    return lax.dot_general(
        left_side, right_side, (((1,), (1,)), ((), ())), preferred_element_type=jnp.float32
    )


def weight_product(left_side, right_side):
    return lax.dot_general(
        left_side, right_side, (((0,), (0,)), ((), ())), preferred_element_type=jnp.float32
    )


def per_device(
    inputs,
    out_grad,
    lengths,
    permutation,
    gain_attention,
    query_weight,
    key_weight,
    value_weight,
    out_weight,
    bucket_bias,
    gain_feedforward,
    gate_weight,
    up_weight,
    down_weight,
):
    gathered = (
        lax.all_gather(query_weight, "wshard", axis=0, tiled=True),
        lax.all_gather(key_weight, "wshard", axis=0, tiled=True),
        lax.all_gather(value_weight, "wshard", axis=0, tiled=True),
        lax.all_gather(out_weight, "wshard", axis=0, tiled=True),
        lax.all_gather(gate_weight, "wshard", axis=0, tiled=True),
        lax.all_gather(up_weight, "wshard", axis=0, tiled=True),
        lax.all_gather(down_weight, "wshard", axis=0, tiled=True),
    )
    query_full, key_full, value_full, out_full, gate_full, up_full, down_full = gathered
    rows = inputs.shape[0]
    buckets = bucket_bias.shape[0]
    heads = bucket_bias.shape[1]
    width = query_weight.shape[1]
    head_size = width // heads
    peers = lax.axis_size(("ctx", "wshard"))
    group_tokens = rows * peers
    breadth = min(512, group_tokens)
    blocks = group_tokens // breadth
    first = lax.axis_index(("ctx", "wshard")) * rows
    seq_ends = jnp.cumsum(lengths[0])
    order_row = permutation[0]
    inverse = (
        jnp.zeros((group_tokens,), jnp.int32).at[order_row].set(lax.iota(jnp.int32, group_tokens))
    )

    def sequence_of(places):
        return jnp.sum((places[:, None] >= seq_ends[None, :]).astype(jnp.int32), axis=1)

    query_place = lax.dynamic_slice_in_dim(order_row, first, rows, 0)
    query_seq = sequence_of(query_place)
    seq_lowest = jnp.min(query_seq)
    seq_highest = jnp.max(query_seq)
    bucket_ids = lax.iota(jnp.int32, buckets)

    def live(key_start):
        key_seq = sequence_of(lax.dynamic_slice_in_dim(order_row, key_start, breadth, 0))
        return (jnp.min(key_seq) <= seq_highest) & (jnp.max(key_seq) >= seq_lowest)

    all_grads = lax.all_gather(out_grad, ("ctx", "wshard"), axis=0, tiled=True)
    dy_rows = jnp.take(all_grads, query_place, axis=0)
    inputs_wide = inputs.astype(jnp.float32)
    normed = rms_norm(inputs_wide, gain_attention).astype(jnp.bfloat16)
    query_proj = forward_product(normed, query_full).astype(jnp.bfloat16)
    key_proj = forward_product(normed, key_full).astype(jnp.bfloat16)
    value_proj = forward_product(normed, value_full).astype(jnp.bfloat16)
    query_heads = query_proj.reshape(rows, heads, head_size)
    key_value = (
        lax.all_gather(key_proj, ("ctx", "wshard"), axis=0, tiled=True),
        lax.all_gather(value_proj, ("ctx", "wshard"), axis=0, tiled=True),
    )

    def block_scores(key_start, key_all):
        key_block = lax.dynamic_slice_in_dim(key_all, key_start, breadth, 0).reshape(
            breadth, heads, head_size
        )
        scores = jnp.einsum(
            "qhd,khd->hqk", query_heads, key_block, preferred_element_type=jnp.float32
        )
        key_place = lax.dynamic_slice_in_dim(order_row, key_start, breadth, 0)
        offsets = key_place[None, :] - query_place[:, None]
        picks = (bucket_of(offsets)[:, :, None] == bucket_ids[None, None, :]).astype(jnp.float32)
        scores = scores + jnp.einsum("qkb,bh->hqk", picks, bucket_bias, precision=highest)
        key_seq = sequence_of(key_place)
        same_seq = (query_seq[:, None] == key_seq[None, :])[None]
        return (jnp.where(same_seq, scores, masked_out), key_block, picks)

    def value_block_of(key_start, value_all):
        return lax.dynamic_slice_in_dim(value_all, key_start, breadth, 0).reshape(
            breadth, heads, head_size
        )

    def visit(step_fn, carry):

        def one_step(block_index, running):
            key_start = block_index * breadth
            return lax.cond(
                live(key_start),
                lambda current: step_fn(key_start, current),
                lambda current: current,
                running,
            )

        return lax.fori_loop(0, blocks, one_step, carry)

    def peak_step(key_start, running):
        top_now, total_now = running
        scores = block_scores(key_start, key_value[0])[0]
        top_next = jnp.maximum(top_now, jnp.max(scores, axis=2))
        total_next = total_now * jnp.exp(top_now - top_next) + jnp.sum(
            jnp.exp(scores - top_next[:, :, None]), axis=2
        )
        return (top_next, total_next)

    start_top = jnp.full((heads, rows), masked_out, jnp.float32)
    top_all, total_all = visit(peak_step, (start_top, jnp.zeros((heads, rows), jnp.float32)))
    log_total = top_all + jnp.log(total_all)

    def value_step(key_start, running):
        scores = block_scores(key_start, key_value[0])[0]
        value_block = value_block_of(key_start, key_value[1])
        probs_low = jnp.exp(scores - log_total[:, :, None]).astype(jnp.bfloat16)
        return running + jnp.einsum(
            "hqk,khd->qhd", probs_low, value_block, preferred_element_type=jnp.float32
        )

    attended_wide = visit(value_step, jnp.zeros((rows, heads, head_size), jnp.float32))
    attended = attended_wide.reshape(rows, width).astype(jnp.bfloat16)
    residual = inputs_wide + forward_product(attended, out_full)
    normed_ff = rms_norm(residual, gain_feedforward).astype(jnp.bfloat16)
    gate_proj = forward_product(normed_ff, gate_full)
    up_proj = forward_product(normed_ff, up_full)

    def activate(gate_in, up_in):
        return jax.nn.gelu(gate_in, approximate=True) * up_in

    hidden_wide, activate_back = jax.vjp(activate, gate_proj, up_proj)
    hidden = hidden_wide.astype(jnp.bfloat16)
    outputs_dealt = (residual + forward_product(hidden, down_full)).astype(jnp.bfloat16)
    later = (
        lax.all_gather(query_weight, "wshard", axis=0, tiled=True),
        lax.all_gather(key_weight, "wshard", axis=0, tiled=True),
        lax.all_gather(value_weight, "wshard", axis=0, tiled=True),
        lax.all_gather(out_weight, "wshard", axis=0, tiled=True),
        lax.all_gather(gate_weight, "wshard", axis=0, tiled=True),
        lax.all_gather(up_weight, "wshard", axis=0, tiled=True),
        lax.all_gather(down_weight, "wshard", axis=0, tiled=True),
    )
    key_value_back = (
        lax.all_gather(key_proj, ("ctx", "wshard"), axis=0, tiled=True),
        lax.all_gather(value_proj, ("ctx", "wshard"), axis=0, tiled=True),
    )
    query_back, key_back, value_back, out_back, gate_back, up_back, down_back = later
    grad_down = weight_product(hidden, dy_rows)
    d_hidden = backward_product(dy_rows, down_back)
    d_gate_wide, d_up_wide = activate_back(d_hidden)
    d_gate = d_gate_wide.astype(jnp.bfloat16)
    d_up = d_up_wide.astype(jnp.bfloat16)
    grad_gate = weight_product(normed_ff, d_gate)
    grad_up = weight_product(normed_ff, d_up)
    d_normed_ff = backward_product(d_gate, gate_back) + backward_product(d_up, up_back)
    norm_ff_back = jax.vjp(rms_norm, residual, gain_feedforward)[1]
    d_residual_norm, grad_gain_ff = norm_ff_back(d_normed_ff)
    d_residual = dy_rows.astype(jnp.float32) + d_residual_norm
    d_branch = d_residual.astype(jnp.bfloat16)
    grad_out = weight_product(attended, d_branch)
    d_attended = backward_product(d_branch, out_back).astype(jnp.bfloat16)
    d_heads = d_attended.reshape(rows, heads, head_size)
    delta = jnp.einsum("qhd,qhd->hq", d_heads.astype(jnp.float32), attended_wide, precision=highest)

    def grad_step(key_start, running):
        d_query_acc, d_keyvalue, d_table = running
        scores, key_block, picks = block_scores(key_start, key_value_back[0])
        value_block = value_block_of(key_start, key_value_back[1])
        soft = jnp.exp(scores - log_total[:, :, None])
        d_probs = jnp.einsum(
            "qhd,khd->hqk", d_heads, value_block, preferred_element_type=jnp.float32
        )
        d_scores = (soft * (d_probs - delta[:, :, None])).astype(jnp.bfloat16)
        d_query_acc = d_query_acc + jnp.einsum(
            "hqk,khd->qhd", d_scores, key_block, preferred_element_type=jnp.float32
        )
        d_key_block = jnp.einsum(
            "hqk,qhd->khd", d_scores, query_heads, preferred_element_type=jnp.float32
        ).reshape(breadth, width)
        d_value_block = jnp.einsum(
            "hqk,qhd->khd", soft.astype(jnp.bfloat16), d_heads, preferred_element_type=jnp.float32
        ).reshape(breadth, width)
        d_keyvalue = lax.dynamic_update_slice_in_dim(
            d_keyvalue, jnp.concatenate([d_key_block, d_value_block], axis=1), key_start, 0
        )
        d_table = d_table + jnp.einsum(
            "qkb,hqk->bh", picks, d_scores.astype(jnp.float32), precision=highest
        )
        return (d_query_acc, d_keyvalue, d_table)

    start_grad = (
        jnp.zeros((rows, heads, head_size), jnp.float32),
        jnp.zeros((group_tokens, 2 * width), jnp.float32),
        jnp.zeros((buckets, heads), jnp.float32),
    )
    d_query_all, d_keyvalue_all, d_table_all = visit(grad_step, start_grad)
    own_keyvalue = lax.psum_scatter(
        d_keyvalue_all.astype(jnp.bfloat16), ("ctx", "wshard"), scatter_dimension=0, tiled=True
    ).astype(jnp.float32)
    d_query = d_query_all.reshape(rows, width).astype(jnp.bfloat16)
    d_key = own_keyvalue[:, :width].astype(jnp.bfloat16)
    d_value = own_keyvalue[:, width:].astype(jnp.bfloat16)
    grad_query = weight_product(normed, d_query)
    grad_key = weight_product(normed, d_key)
    grad_value = weight_product(normed, d_value)
    d_normed = (
        backward_product(d_query, query_back)
        + backward_product(d_key, key_back)
        + backward_product(d_value, value_back)
    )
    norm_attn_back = jax.vjp(rms_norm, inputs_wide, gain_attention)[1]
    d_input_norm, grad_gain_attn = norm_attn_back(d_normed)
    input_grad_dealt = (d_residual + d_input_norm).astype(jnp.bfloat16)
    grad_table = lax.psum(d_table_all, ("group", "ctx", "wshard"))
    returned = (
        lax.all_gather(outputs_dealt, ("ctx", "wshard"), axis=0, tiled=True),
        lax.all_gather(input_grad_dealt, ("ctx", "wshard"), axis=0, tiled=True),
    )
    own_rows = lax.dynamic_slice_in_dim(inverse, first, rows, 0)
    outputs = jnp.take(returned[0], own_rows, axis=0)
    input_grad = jnp.take(returned[1], own_rows, axis=0)
    shares = (
        lax.psum_scatter(
            grad_gain_attn.astype(jnp.bfloat16), ("ctx", "wshard"), scatter_dimension=0, tiled=True
        ).astype(jnp.float32),
        lax.psum_scatter(
            grad_query.astype(jnp.bfloat16), ("ctx", "wshard"), scatter_dimension=0, tiled=True
        ).astype(jnp.float32),
        lax.psum_scatter(
            grad_key.astype(jnp.bfloat16), ("ctx", "wshard"), scatter_dimension=0, tiled=True
        ).astype(jnp.float32),
        lax.psum_scatter(
            grad_value.astype(jnp.bfloat16), ("ctx", "wshard"), scatter_dimension=0, tiled=True
        ).astype(jnp.float32),
        lax.psum_scatter(
            grad_out.astype(jnp.bfloat16), ("ctx", "wshard"), scatter_dimension=0, tiled=True
        ).astype(jnp.float32),
        lax.psum_scatter(
            grad_gain_ff.astype(jnp.bfloat16), ("ctx", "wshard"), scatter_dimension=0, tiled=True
        ).astype(jnp.float32),
        lax.psum_scatter(
            grad_gate.astype(jnp.bfloat16), ("ctx", "wshard"), scatter_dimension=0, tiled=True
        ).astype(jnp.float32),
        lax.psum_scatter(
            grad_up.astype(jnp.bfloat16), ("ctx", "wshard"), scatter_dimension=0, tiled=True
        ).astype(jnp.float32),
        lax.psum_scatter(
            grad_down.astype(jnp.bfloat16), ("ctx", "wshard"), scatter_dimension=1, tiled=True
        ).astype(jnp.float32),
    )
    totals = (
        lax.psum(shares[0].astype(jnp.bfloat16), "group").astype(jnp.float32),
        lax.psum(shares[1].astype(jnp.bfloat16), "group").astype(jnp.float32),
        lax.psum(shares[2].astype(jnp.bfloat16), "group").astype(jnp.float32),
        lax.psum(shares[3].astype(jnp.bfloat16), "group").astype(jnp.float32),
        lax.psum(shares[4].astype(jnp.bfloat16), "group").astype(jnp.float32),
        lax.psum(shares[5].astype(jnp.bfloat16), "group").astype(jnp.float32),
        lax.psum(shares[6].astype(jnp.bfloat16), "group").astype(jnp.float32),
        lax.psum(shares[7].astype(jnp.bfloat16), "group").astype(jnp.float32),
        lax.psum(shares[8].astype(jnp.bfloat16), "group").astype(jnp.float32),
    )
    return (
        outputs,
        input_grad,
        totals[0],
        totals[1],
        totals[2],
        totals[3],
        totals[4],
        grad_table,
        totals[5],
        totals[6],
        totals[7],
        totals[8],
    )


def solution(mesh):
    return jax.shard_map(
        per_device,
        mesh=mesh,
        in_specs=(
            P(("group", "ctx", "wshard"), None),
            P(("group", "ctx", "wshard"), None),
            P("group", None),
            P("group", None),
            P(),
            P("wshard", None),
            P("wshard", None),
            P("wshard", None),
            P("wshard", None),
            P(),
            P(),
            P("wshard", None),
            P("wshard", None),
            P("wshard", None),
        ),
        out_specs=(
            P(("group", "ctx", "wshard"), None),
            P(("group", "ctx", "wshard"), None),
            P(("ctx", "wshard")),
            P(("ctx", "wshard"), None),
            P(("ctx", "wshard"), None),
            P(("ctx", "wshard"), None),
            P(("ctx", "wshard"), None),
            P(),
            P(("ctx", "wshard")),
            P(("ctx", "wshard"), None),
            P(("ctx", "wshard"), None),
            P(None, ("ctx", "wshard")),
        ),
        check_vma=False,
    )
```

profile of v0, /device:TPU:0, one launch (start us, length us, event | category | flops | bytes accessed | tf_op | source)
XLA Modules:
  0.0 1275.2 jit_solution(9304477346111395155)
XLA Ops:
  9.7 13.5 %all-gather.13.cloned.1.call-done = bf16[1536,768]{1,0:T(8,128)(2,1)} async-done(((bf16[768,768]{1,0:T(8,128)(2,1)}), bf16[1536,768]{1,0:T(8,128)(2,1)}) %all-gather.13.cloned.1.call-update) | async-done | bytes 2359312 | tf_op jit(solution)/shard_map/all_gather | solution.py:62
  53.4 20.2 %all-gather.15.cloned.1.call-done = bf16[1024,768]{1,0:T(8,128)(2,1)} async-done(((bf16[256,768]{1,0:T(8,128)(2,1)}), bf16[1024,768]{1,0:T(8,128)(2,1)}) %all-gather.15.cloned.1.call-update) | async-done | bytes 1572880 | tf_op jit(solution)/shard_map/all_gather | solution.py:108
  75.3 19.9 %all-gather.19.cloned.1.call-done = bf16[1024,768]{1,0:T(8,128)(2,1)} async-done(((bf16[256,768]{1,0:T(8,128)(2,1)}), bf16[1024,768]{1,0:T(8,128)(2,1)}) %all-gather.19.cloned.1.call-update) | async-done | bytes 1572880 | tf_op jit(solution)/shard_map/all_gather | solution.py:107
  97.6 65.7 %while.51 = (s32[]{:T(128)}, f32[12,256]{1,0:T(8,128)S(1)}, f32[12,256]{1,0:T(8,128)}, s32[1024]{0:T(1024)}, s32[4]{0:T(128)}, /*index=5*/s32[]{:T(128)}, s32[]{...) while((s32[]{:T(128)}, f32[12,256]{1,0:T(8,128)S(1)}, ...), condition=%wide.region_14.15_spmd.clone, body=%wide.region_5.14_spmd.clone.sunk | while | flops 821184512 | bytes 42105104 | solution.py:142
  102.7 26.9 %conditional.9 = ((f32[12,256]{1,0:T(8,128)S(1)}, f32[12,256]{1,0:T(8,128)})) conditional(s32[]{:T(128)} %convert_element_type.489, (f32[12,256]{1,0:T(8,128)S(1)}, f32[12,256]{1,0:T(8,128)}) %tuple.152, (s32[256]{0:T(256)}, s32[]{:T(128)}, s32[1024]{0:T(1024)}, s32[4]{0:T(128)}, bf16[1024,768]{0,1:T(8,128)(2,1)S(1)}, ...), branch_computations={%region_9.9_spmd, %region_10.13_spmd} | conditional | flops 821177856 | bytes 42094376 | solution.py:135
  134.7 28.6 %conditional.9 = ((f32[12,256]{1,0:T(8,128)S(1)}, f32[12,256]{1,0:T(8,128)})) conditional(s32[]{:T(128)} %convert_element_type.489, (f32[12,256]{1,0:T(8,128)S(1)}, f32[12,256]{1,0:T(8,128)}) %tuple.152, (s32[256]{0:T(256)}, s32[]{:T(128)}, s32[1024]{0:T(1024)}, s32[4]{0:T(128)}, bf16[1024,768]{0,1:T(8,128)(2,1)S(1)}, ...), branch_computations={%region_9.9_spmd, %region_10.13_spmd} | conditional | flops 821177856 | bytes 42094376 | solution.py:135
  165.5 67.1 %while.52 = (s32[]{:T(128)}, f32[256,12,64]{0,2,1:T(8,128)}, s32[1024]{0:T(1024)}, s32[4]{0:T(128)}, s32[]{:T(128)}, /*index=5*/s32[]{:T(128)}, bf16[1024,768]{0...) while((s32[]{:T(128)}, f32[256,12,64]{0,2,1:T(8,128)}, ...), condition=%wide.region_22.23_spmd.clone, body=%wide.region_15.22_spmd.clone.sunk | while | flops 1021128704 | bytes 33284948 | solution.py:142
  171.1 28.5 %conditional.10 = (f32[256,12,64]{0,2,1:T(8,128)}) conditional(s32[]{:T(128)} %convert_element_type.491, f32[256,12,64]{0,2,1:T(8,128)} %get-tuple-element.1644, (s32[]{:T(128)}, bf16[1024,768]{0,1:T(8,128)(2,1)S(1)}, s32[256]{0:T(256)}, s32[1024]{0:T(1024)}, s32[4]{0:T(128)}, /*index=5*/bf16[1024,768]{0,1:T(8,128)(2,1)S(1)}, ...), branch_computations={%region_19.19_spmd, %region_20.21_spmd} | conditional | flops 1021122048 | bytes 33274218 | solution.py:135
  204.8 27.7 %conditional.10 = (f32[256,12,64]{0,2,1:T(8,128)}) conditional(s32[]{:T(128)} %convert_element_type.491, f32[256,12,64]{0,2,1:T(8,128)} %get-tuple-element.1644, (s32[]{:T(128)}, bf16[1024,768]{0,1:T(8,128)(2,1)S(1)}, s32[256]{0:T(256)}, s32[1024]{0:T(1024)}, s32[4]{0:T(128)}, /*index=5*/bf16[1024,768]{0,1:T(8,128)(2,1)S(1)}, ...), branch_computations={%region_19.19_spmd, %region_20.21_spmd} | conditional | flops 1021122048 | bytes 33274218 | solution.py:135
  297.1 52.5 %while.53 = (s32[]{:T(128)}, f32[256,12,64]{0,2,1:T(8,128)S(1)}, bf16[1024,1536]{0,1:T(8,128)(2,1)}, f32[32,12]{0,1:T(8,128)S(1)}, s32[1024]{0:T(1024)S(1)}, /*i...) while((s32[]{:T(128)}, f32[256,12,64]{0,2,1:T(8,128)S(1)}, ...), condition=%wide.region_33.35_spmd.clone, body=%wide.region_26.0_spmd.clone.sunk | while | flops 1737830784 | bytes 84465112 | solution.py:142
  300.8 22.6 %conditional.11 = ((f32[256,12,64]{0,2,1:T(8,128)S(1)}, bf16[1024,1536]{0,1:T(8,128)(2,1)}, f32[32,12]{0,1:T(8,128)S(1)})) conditional(s32[]{:T(128)} %convert_element_type.493, (f32[256,12,64]{0,2,1:T(8,128)S(1)}, bf16[1024,1536]{0,1:T(8,128)(2,1)}, f32[32,12]{0,1:T(8,128)S(1)}) %tuple.159, (s32[]{:T(128)}, bf16[1024,768]{0,1:T(8,128)(2,1)S(1)}, ...), branch_computations={%region_30.31_spmd, %region_31.33_spmd} | conditional | flops 1737824128 | bytes 84454296 | solution.py:135
  326.8 22.6 %conditional.11 = ((f32[256,12,64]{0,2,1:T(8,128)S(1)}, bf16[1024,1536]{0,1:T(8,128)(2,1)}, f32[32,12]{0,1:T(8,128)S(1)})) conditional(s32[]{:T(128)} %convert_element_type.493, (f32[256,12,64]{0,2,1:T(8,128)S(1)}, bf16[1024,1536]{0,1:T(8,128)(2,1)}, f32[32,12]{0,1:T(8,128)S(1)}) %tuple.159, (s32[]{:T(128)}, bf16[1024,768]{0,1:T(8,128)(2,1)S(1)}, ...), branch_computations={%region_30.31_spmd, %region_31.33_spmd} | conditional | flops 1737824128 | bytes 84454296 | solution.py:135
  359.4 16.2 %copy.97 = bf16[3968,1536]{0,1:T(8,128)(2,1)} copy(bf16[3968,1536]{1,0:T(8,128)(2,1)} %convolution_convert_fusion) | data formatting | bytes 24379392
  395.4 11.9 convolution_convert_fusion.2
  433.6 54.4 %reduce-scatter.25.cloned.1.call-done = bf16[384,3968]{1,0:T(8,128)(2,1)} async-done(((bf16[1536,3968]{1,0:T(8,128)(2,1)}), bf16[384,3968]{1,0:T(8,128)(2,1)}) %reduce-scatter.25.cloned.1.call-update) | async-done | bytes 3047440
  492.5 31.4 %reduce-scatter.13.cloned.1.call-done = bf16[384,768]{1,0:T(8,128)(2,1)} async-done(((bf16[1536,768]{1,0:T(8,128)(2,1)}), bf16[384,768]{1,0:T(8,128)(2,1)}) %reduce-scatter.13.cloned.1.call-update) | async-done | bytes 589840 | tf_op jit(solution)/shard_map/reduce_scatter | solution.py:270
  523.9 35.2 %reduce-scatter.19.cloned.1.call-done = bf16[192,1536]{1,0:T(8,128)(2,1)} async-done(((bf16[768,1536]{1,0:T(8,128)(2,1)}), bf16[192,1536]{1,0:T(8,128)(2,1)}) %reduce-scatter.19.cloned.1.call-update) | async-done | bytes 589840 | tf_op jit(solution)/shard_map/reduce_scatter | solution.py:279
  559.1 35.8 %reduce-scatter.15.cloned.1.call-done = bf16[384,768]{1,0:T(8,128)(2,1)} async-done(((bf16[1536,768]{1,0:T(8,128)(2,1)}), bf16[384,768]{1,0:T(8,128)(2,1)}) %reduce-scatter.15.cloned.1.call-update) | async-done | bytes 589840 | tf_op jit(solution)/shard_map/reduce_scatter | solution.py:273
  595.0 35.2 %reduce-scatter.17.cloned.1.call-done = bf16[384,768]{1,0:T(8,128)(2,1)} async-done(((bf16[1536,768]{1,0:T(8,128)(2,1)}), bf16[384,768]{1,0:T(8,128)(2,1)}) %reduce-scatter.17.cloned.1.call-update) | async-done | bytes 589840 | tf_op jit(solution)/shard_map/reduce_scatter | solution.py:276
  630.2 99.5 %reduce-scatter.21.cloned.1.call-done = bf16[384,3968]{1,0:T(8,128)(2,1)} async-done(((bf16[1536,3968]{1,0:T(8,128)(2,1)}), bf16[384,3968]{1,0:T(8,128)(2,1)}) %reduce-scatter.21.cloned.1.call-update) | async-done | bytes 3047440 | tf_op jit(solution)/shard_map/reduce_scatter | solution.py:285
  729.7 99.5 %reduce-scatter.23.cloned.1.call-done = bf16[384,3968]{1,0:T(8,128)(2,1)} async-done(((bf16[1536,3968]{1,0:T(8,128)(2,1)}), bf16[384,3968]{1,0:T(8,128)(2,1)}) %reduce-scatter.23.cloned.1.call-update) | async-done | bytes 3047440 | tf_op jit(solution)/shard_map/reduce_scatter | solution.py:288
  835.0 39.9 %psum.75 = f32[32,12]{0,1:T(8,128)} all-reduce(f32[32,12]{0,1:T(8,128)S(1)} %copy-done.48), channel_id=1, replica_groups=mesh['group'=8,'ctx'=2,'wshard'=2] {'group','ctx','wshard'}, use_global_device_ids=true, to_apply=%region_47.49 | all-reduce | flops 384 | bytes 3072 | tf_op jit(solution)/shard_map/psum | solution.py:258
  887.7 19.8 %all-reduce.2 = (bf16[384]{0:T(512)(128)(2,1)S(1)}, bf16[384]{0:T(512)(128)(2,1)S(1)}) all-reduce(bf16[384]{0:T(512)(128)(2,1)S(1)} %dynamic-slice.2, bf16[384]{0:T(512)(128)(2,1)S(1)} %dynamic-slice.4), channel_id=1, replica_groups=mesh['group'=8,'ctx'=2,'wshard'=2] {'group'}, use_global_device_ids=true, to_apply=%region_38.40 | all-reduce | flops 768 | bytes 3072 | tf_op jit(solution)/shard_map/psum | solution.py:296
  914.3 337.8 %all-reduce.7.cloned.1.call-done = (bf16[384,768]{1,0:T(8,128)(2,1)}, bf16[384,768]{1,0:T(8,128)(2,1)}, bf16[384,768]{1,0:T(8,128)(2,1)}, bf16[192,1536]{1,0:T(8...) async-done(((bf16[384,768]{1,0:T(8,128)(2,1)}, bf16[384,768]{1,0:T(8,128)(2,1)}, bf16[384,768]{1,0:T(8,128)(2,1)}, ...) | async-done | bytes 11501584 | tf_op jit(solution)/shard_map/psum | solution.py:297
  (348 shorter events, 372.1 us)
Async XLA Ops:
  7.2 16.1 %all-gather.13.cloned.1.call-start = ((), (), s32[]{:S(2)}) async-start(), calls=%async_computation.8 | async-start | bytes 3538944 | tf_op jit(solution)/shard_map/all_gather | solution.py:62
  7.9 29.0 %all-gather.17.cloned.1.call-start = ((), (), s32[]{:S(2)}) async-start(), calls=%async_computation.10 | async-start | bytes 3538944 | tf_op jit(solution)/shard_map/all_gather | solution.py:61
  8.7 42.1 %all-gather.21.cloned.1.call-start = ((), (), s32[]{:S(2)}) async-start(), calls=%async_computation.12 | async-start | bytes 3538944 | tf_op jit(solution)/shard_map/all_gather | solution.py:60
  9.4 64.2 %all-gather.15.cloned.1.call-start = ((), (), s32[]{:S(2)}) async-start(), calls=%async_computation.9 | async-start | bytes 1966080 | tf_op jit(solution)/shard_map/all_gather | solution.py:108
  9.7 16.8 %copy-start.49 = (f32[256]{0:T(256)}, f32[256]{0:T(256)S(1)}, u32[]{:S(2)}) copy-start(f32[256]{0:T(256)S(1)} %fusion.99) | copy-start | bytes 3076
  9.7 41.0 %copy-start.44 = (f32[256]{0:T(256)}, f32[256]{0:T(256)S(1)}, u32[]{:S(2)}) copy-start(f32[256]{0:T(256)S(1)} %fusion.110) | copy-start | bytes 3076
  26.5 68.7 %all-gather.19.cloned.1.call-start = ((), (), s32[]{:S(2)}) async-start(), calls=%async_computation.11 | async-start | bytes 1966080 | tf_op jit(solution)/shard_map/all_gather | solution.py:107
  40.3 194.9 %all-gather.33.cloned.1.call-start = ((), (), s32[]{:S(2)}) async-start(), calls=%async_computation.18 | async-start | bytes 3932160 | tf_op jit(solution)/shard_map/all_gather | solution.py:98
  40.8 199.6 %all-gather.23.cloned.1.call-start = ((), (), s32[]{:S(2)}) async-start(), calls=%async_computation.13 | async-start | bytes 3538944 | tf_op jit(solution)/shard_map/all_gather | solution.py:63
  41.6 203.1 %all-gather.25.cloned.1.call-start = ((), (), s32[]{:S(2)}) async-start(), calls=%async_computation.14 | async-start | bytes 18284544 | tf_op jit(solution)/shard_map/all_gather | solution.py:64
  42.3 212.4 %all-gather.27.cloned.1.call-start = ((), (), s32[]{:S(2)}) async-start(), calls=%async_computation.15 | async-start | bytes 18284544 | tf_op jit(solution)/shard_map/all_gather | solution.py:65
  43.1 221.8 %all-gather.29.cloned.1.call-start = ((), (), s32[]{:S(2)}) async-start(), calls=%async_computation.16 | async-start | bytes 18284544 | tf_op jit(solution)/shard_map/all_gather | solution.py:66
  43.7 344.8 %reduce-scatter.11.cloned.1.call-start = ((), (), s32[]{:S(2)}) async-start(), calls=%async_computation.19 | async-start | bytes 3932160 | tf_op jit(solution)/shard_map/reduce_scatter | solution.py:241
  243.3 48.2 %copy-start.5 = (f32[256,1536]{1,0:T(8,128)}, f32[256,1536]{1,0:T(8,128)S(1)}, u32[]{:S(2)}) copy-start(f32[256,1536]{1,0:T(8,128)S(1)} %get-tuple-element.1288) | copy-start | bytes 4718596
  349.6 138.4 %reduce-scatter.25.cloned.1.call-start = ((), (), s32[]{:S(2)}) async-start(), calls=%async_computation.27 | async-start | bytes 15237120
  375.6 148.3 %reduce-scatter.13.cloned.1.call-start = ((), (), s32[]{:S(2)}) async-start(), calls=%async_computation.21 | async-start | bytes 2949120 | tf_op jit(solution)/shard_map/reduce_scatter | solution.py:270
  379.1 180.0 %reduce-scatter.19.cloned.1.call-start = ((), (), s32[]{:S(2)}) async-start(), calls=%async_computation.24 | async-start | bytes 2949120 | tf_op jit(solution)/shard_map/reduce_scatter | solution.py:279
  381.4 213.5 %reduce-scatter.15.cloned.1.call-start = ((), (), s32[]{:S(2)}) async-start(), calls=%async_computation.22 | async-start | bytes 2949120 | tf_op jit(solution)/shard_map/reduce_scatter | solution.py:273
  391.8 238.4 %reduce-scatter.17.cloned.1.call-start = ((), (), s32[]{:S(2)}) async-start(), calls=%async_computation.23 | async-start | bytes 2949120 | tf_op jit(solution)/shard_map/reduce_scatter | solution.py:276
  395.3 334.4 %reduce-scatter.21.cloned.1.call-start = ((), (), s32[]{:S(2)}) async-start(), calls=%async_computation.25 | async-start | bytes 15237120 | tf_op jit(solution)/shard_map/reduce_scatter | solution.py:285
  407.4 421.9 %reduce-scatter.23.cloned.1.call-start = ((), (), s32[]{:S(2)}) async-start(), calls=%async_computation.26 | async-start | bytes 15237120 | tf_op jit(solution)/shard_map/reduce_scatter | solution.py:288
  415.5 459.4 %all-gather.31.cloned.1.call-start = ((), (), s32[]{:S(2)}) async-start(), calls=%async_computation.17 | async-start | bytes 3932160 | tf_op jit(solution)/shard_map/all_gather | solution.py:260
  426.3 482.3 %all-gather.35.cloned.1.call-start = ((), (), s32[]{:S(2)}) async-start(), calls=%async_computation.20 | async-start | bytes 3932160 | tf_op jit(solution)/shard_map/all_gather | solution.py:261
  433.5 818.5 %all-reduce.7.cloned.1.call-start = ((), (), s32[]{:S(2)}) async-start(), calls=%async_computation.28 | async-start | bytes 23003136 | tf_op jit(solution)/shard_map/psum | solution.py:297
  (64 other events, 211.0 us)
Sparse Core Ops, SparseCore 0:
  9.5 13.6 all-gather.12
  24.8 12.1 all-gather.16
  38.5 12.1 all-gather.20
  52.7 20.8 all-gather.14
  75.6 19.6 all-gather.18
  96.6 28.4 all-gather.32
  126.7 10.9 all-gather.22
  139.3 25.4 all-gather.24
  166.3 25.4 all-gather.26
  193.3 25.5 all-gather.28
  349.7 38.6 reduce-scatter.10
  390.9 96.9 reduce-scatter.24
  491.1 32.8 reduce-scatter.12
  526.3 32.8 reduce-scatter.18
  562.1 32.8 reduce-scatter.14
  597.3 32.8 reduce-scatter.16
  632.6 97.0 reduce-scatter.20
  732.2 97.0 reduce-scatter.22
  831.4 29.0 all-gather.30
  862.4 29.0 all-gather.34
  897.7 354.3 all-reduce.6
where the time goes:
time: 1290 us; the launch traced here: 1280 us
  waiting for transfers between devices  809 us (63%)
  matrix products  202 us (16%)
  local copies, waits for them, and re-layouts  113 us (9%)
  blocking collectives  67.9 us (5%)
  other arithmetic  49.9 us (4%)
  loops' own time  16.9 us (1%)
  between operations  15.8 us (1%)
    psum x1, waiting for transfers between devices, per_device(): lax.psum(shares[1].astype(jnp.bfloat16), 'group').astype(jnp.float32)  338 us
    reduce_scatter x1, waiting for transfers between devices, per_device(): lax.psum_scatter(grad_up.astype(jnp.bfloat16), ('ctx', 'wshard'), scatter...  99.5 us
    reduce_scatter x1, waiting for transfers between devices, per_device(): lax.psum_scatter(grad_gate.astype(jnp.bfloat16), ('ctx', 'wshard'), scatt...  99.5 us
    unnamed x22, waiting for transfers between devices  59.8 us
    dot_general x7, matrix products, forward_product(): return jnp.dot(left_side, right_side, preferred_element_type=jnp.float32)  42.8 us
    dot_general x6, matrix products, block_scores(): jnp.einsum('qkb,bh->hqk', picks, bucket_bias, precision=highest)  40.7 us
    psum x1, blocking collectives, per_device(): grad_table = lax.psum(d_table_all, ('group', 'ctx', 'wshard'))  39.9 us
    dot_general x7, matrix products, weight_product(): lax.dot_general(left_side, right_side, (((0,), (0,)), ((), ())), preferre...  39.9 us
  transfers between devices with their start and end apart: 21, of which 14 were waited for; matrix products, arithmetic and copies ran while one was open for 21% of the time, Pallas kernels for 0%

commit v1 on v0

--- a/solution.py
+++ b/solution.py
@@ -7,6 +7,12 @@
 highest = lax.Precision.HIGHEST
 thresholds = (12, 16, 23, 32, 46, 64, 91)
 masked_out = -1e30
+
+
+def gather_and_add(array, axis):
+    parts = lax.all_gather(array, axis, axis=0, tiled=False)
+    total = parts.sum(axis=0)
+    return total
 
 
 def bucket_of(offset):
@@ -294,7 +300,7 @@
     )
     totals = (
         lax.psum(shares[0].astype(jnp.bfloat16), "group").astype(jnp.float32),
-        lax.psum(shares[1].astype(jnp.bfloat16), "group").astype(jnp.float32),
+        gather_and_add(shares[1].astype(jnp.bfloat16), "group").astype(jnp.float32),
         lax.psum(shares[2].astype(jnp.bfloat16), "group").astype(jnp.float32),
         lax.psum(shares[3].astype(jnp.bfloat16), "group").astype(jnp.float32),
         lax.psum(shares[4].astype(jnp.bfloat16), "group").astype(jnp.float32),

time: 1290 us -> 1350 us (1.047)
  waiting for transfers between devices: 809 us -> 873 us
    all_gather x0 -> x1, waiting for transfers between devices: none -> 58.3 us  [gather_and_add(): parts = lax.all_gather(array, axis, axis=0, tiled=False)]
    unnamed x22 -> x23, waiting for transfers between devices: 59.8 us -> 101 us
    reduce_scatter x1, waiting for transfers between devices: 31.4 us -> 0.02 us  [per_device(): lax.psum_scatter(grad_query.astype(jnp.bfloat16), ('ctx', 'wshard'), scat...]
    unnamed x97 -> x95, local copies, waits for them, and re-layouts: 30.5 us -> 30.5 us
  transfers between devices with their start and end apart: 21 -> 22, of which waited for: 14 -> 14; matrix products, arithmetic and copies ran while one was open for 21% -> 20% of each run, Pallas kernels for 0% -> 0%
where the time goes in v1:
time: 1350 us; the launch traced here: 1340 us
  waiting for transfers between devices  873 us (65%)
  matrix products  197 us (15%)
  local copies, waits for them, and re-layouts  113 us (8%)
  blocking collectives  68.2 us (5%)
  other arithmetic  53.2 us (4%)
  loops' own time  17 us (1%)
  between operations  15.9 us (1%)
    psum x1, waiting for transfers between devices, per_device(): lax.psum(shares[2].astype(jnp.bfloat16), 'group').astype(jnp.float32)  338 us
    unnamed x23, waiting for transfers between devices  101 us
    reduce_scatter x1, waiting for transfers between devices, per_device(): lax.psum_scatter(grad_gate.astype(jnp.bfloat16), ('ctx', 'wshard'), scatt...  99.5 us
    reduce_scatter x1, waiting for transfers between devices, per_device(): lax.psum_scatter(grad_up.astype(jnp.bfloat16), ('ctx', 'wshard'), scatter...  99.5 us
    all_gather x1, waiting for transfers between devices, gather_and_add(): parts = lax.all_gather(array, axis, axis=0, tiled=False)  58.3 us
    dot_general x7, matrix products, forward_product(): return jnp.dot(left_side, right_side, preferred_element_type=jnp.float32)  41.8 us
    dot_general x6, matrix products, block_scores(): jnp.einsum('qkb,bh->hqk', picks, bucket_bias, precision=highest)  40.7 us
    psum x1, blocking collectives, per_device(): grad_table = lax.psum(d_table_all, ('group', 'ctx', 'wshard'))  39.9 us
  transfers between devices with their start and end apart: 22, of which 14 were waited for; matrix products, arithmetic and copies ran while one was open for 20% of the time, Pallas kernels for 0%

profile of v1, /device:TPU:0, one launch (start us, length us, event | category | flops | bytes accessed | tf_op | source)
XLA Modules:
  0.0 1337.5 jit_solution(5522717260750364298)
XLA Ops:
  9.7 13.5 %all-gather.15.cloned.1.call-done = bf16[1536,768]{1,0:T(8,128)(2,1)} async-done(((bf16[768,768]{1,0:T(8,128)(2,1)}), bf16[1536,768]{1,0:T(8,128)(2,1)}) %all-gather.15.cloned.1.call-update) | async-done | bytes 2359312 | tf_op jit(solution)/shard_map/all_gather | solution.py:68
  53.4 20.2 %all-gather.17.cloned.1.call-done = bf16[1024,768]{1,0:T(8,128)(2,1)} async-done(((bf16[256,768]{1,0:T(8,128)(2,1)}), bf16[1024,768]{1,0:T(8,128)(2,1)}) %all-gather.17.cloned.1.call-update) | async-done | bytes 1572880 | tf_op jit(solution)/shard_map/all_gather | solution.py:114
  75.3 19.9 %all-gather.21.cloned.1.call-done = bf16[1024,768]{1,0:T(8,128)(2,1)} async-done(((bf16[256,768]{1,0:T(8,128)(2,1)}), bf16[1024,768]{1,0:T(8,128)(2,1)}) %all-gather.21.cloned.1.call-update) | async-done | bytes 1572880 | tf_op jit(solution)/shard_map/all_gather | solution.py:113
  97.6 65.7 %while.51 = (s32[]{:T(128)}, f32[12,256]{1,0:T(8,128)S(1)}, f32[12,256]{1,0:T(8,128)}, s32[1024]{0:T(1024)}, s32[4]{0:T(128)}, /*index=5*/s32[]{:T(128)}, s32[]{...) while((s32[]{:T(128)}, f32[12,256]{1,0:T(8,128)S(1)}, ...), condition=%wide.region_14.15_spmd.clone, body=%wide.region_5.14_spmd.clone.sunk | while | flops 821184512 | bytes 42105104 | solution.py:148
  102.7 26.8 %conditional.9 = ((f32[12,256]{1,0:T(8,128)S(1)}, f32[12,256]{1,0:T(8,128)})) conditional(s32[]{:T(128)} %convert_element_type.491, (f32[12,256]{1,0:T(8,128)S(1)}, f32[12,256]{1,0:T(8,128)}) %tuple.152, (s32[256]{0:T(256)}, s32[]{:T(128)}, s32[1024]{0:T(1024)}, s32[4]{0:T(128)}, bf16[1024,768]{0,1:T(8,128)(2,1)S(1)}, ...), branch_computations={%region_9.9_spmd, %region_10.13_spmd} | conditional | flops 821177856 | bytes 42094376 | solution.py:141
  134.7 28.5 %conditional.9 = ((f32[12,256]{1,0:T(8,128)S(1)}, f32[12,256]{1,0:T(8,128)})) conditional(s32[]{:T(128)} %convert_element_type.491, (f32[12,256]{1,0:T(8,128)S(1)}, f32[12,256]{1,0:T(8,128)}) %tuple.152, (s32[256]{0:T(256)}, s32[]{:T(128)}, s32[1024]{0:T(1024)}, s32[4]{0:T(128)}, bf16[1024,768]{0,1:T(8,128)(2,1)S(1)}, ...), branch_computations={%region_9.9_spmd, %region_10.13_spmd} | conditional | flops 821177856 | bytes 42094376 | solution.py:141
  165.5 67.3 %while.52 = (s32[]{:T(128)}, f32[256,12,64]{0,2,1:T(8,128)}, s32[1024]{0:T(1024)}, s32[4]{0:T(128)}, s32[]{:T(128)}, /*index=5*/s32[]{:T(128)}, bf16[1024,768]{0...) while((s32[]{:T(128)}, f32[256,12,64]{0,2,1:T(8,128)}, ...), condition=%wide.region_22.23_spmd.clone, body=%wide.region_15.22_spmd.clone.sunk | while | flops 1021128704 | bytes 33284948 | solution.py:148
  171.2 28.5 %conditional.10 = (f32[256,12,64]{0,2,1:T(8,128)}) conditional(s32[]{:T(128)} %convert_element_type.493, f32[256,12,64]{0,2,1:T(8,128)} %get-tuple-element.1643, (s32[]{:T(128)}, bf16[1024,768]{0,1:T(8,128)(2,1)S(1)}, s32[256]{0:T(256)}, s32[1024]{0:T(1024)}, s32[4]{0:T(128)}, /*index=5*/bf16[1024,768]{0,1:T(8,128)(2,1)S(1)}, ...), branch_computations={%region_19.19_spmd, %region_20.21_spmd} | conditional | flops 1021122048 | bytes 33274218 | solution.py:141
  205.0 27.7 %conditional.10 = (f32[256,12,64]{0,2,1:T(8,128)}) conditional(s32[]{:T(128)} %convert_element_type.493, f32[256,12,64]{0,2,1:T(8,128)} %get-tuple-element.1643, (s32[]{:T(128)}, bf16[1024,768]{0,1:T(8,128)(2,1)S(1)}, s32[256]{0:T(256)}, s32[1024]{0:T(1024)}, s32[4]{0:T(128)}, /*index=5*/bf16[1024,768]{0,1:T(8,128)(2,1)S(1)}, ...), branch_computations={%region_19.19_spmd, %region_20.21_spmd} | conditional | flops 1021122048 | bytes 33274218 | solution.py:141
  265.1 11.3 multiply_convert_fusion
  297.3 52.5 %while.53 = (s32[]{:T(128)}, f32[256,12,64]{0,2,1:T(8,128)S(1)}, bf16[1024,1536]{0,1:T(8,128)(2,1)}, f32[32,12]{0,1:T(8,128)S(1)}, s32[1024]{0:T(1024)S(1)}, /*i...) while((s32[]{:T(128)}, f32[256,12,64]{0,2,1:T(8,128)S(1)}, ...), condition=%wide.region_33.35_spmd.clone, body=%wide.region_26.0_spmd.clone.sunk | while | flops 1737830784 | bytes 84465112 | solution.py:148
  301.0 22.6 %conditional.11 = ((f32[256,12,64]{0,2,1:T(8,128)S(1)}, bf16[1024,1536]{0,1:T(8,128)(2,1)}, f32[32,12]{0,1:T(8,128)S(1)})) conditional(s32[]{:T(128)} %convert_element_type.495, (f32[256,12,64]{0,2,1:T(8,128)S(1)}, bf16[1024,1536]{0,1:T(8,128)(2,1)}, f32[32,12]{0,1:T(8,128)S(1)}) %tuple.159, (s32[]{:T(128)}, bf16[1024,768]{0,1:T(8,128)(2,1)S(1)}, ...), branch_computations={%region_30.31_spmd, %region_31.33_spmd} | conditional | flops 1737824128 | bytes 84454296 | solution.py:141
  327.0 22.6 %conditional.11 = ((f32[256,12,64]{0,2,1:T(8,128)S(1)}, bf16[1024,1536]{0,1:T(8,128)(2,1)}, f32[32,12]{0,1:T(8,128)S(1)})) conditional(s32[]{:T(128)} %convert_element_type.495, (f32[256,12,64]{0,2,1:T(8,128)S(1)}, bf16[1024,1536]{0,1:T(8,128)(2,1)}, f32[32,12]{0,1:T(8,128)S(1)}) %tuple.159, (s32[]{:T(128)}, bf16[1024,768]{0,1:T(8,128)(2,1)S(1)}, ...), branch_computations={%region_30.31_spmd, %region_31.33_spmd} | conditional | flops 1737824128 | bytes 84454296 | solution.py:141
  361.7 15.9 %copy.97 = bf16[3968,1536]{0,1:T(8,128)(2,1)} copy(bf16[3968,1536]{1,0:T(8,128)(2,1)} %convolution_convert_fusion) | data formatting | bytes 24379392
  429.4 94.7 %reduce-scatter.25.cloned.1.call-done = bf16[384,3968]{1,0:T(8,128)(2,1)} async-done(((bf16[1536,3968]{1,0:T(8,128)(2,1)}), bf16[384,3968]{1,0:T(8,128)(2,1)}) %reduce-scatter.25.cloned.1.call-update) | async-done | bytes 3047440
  528.6 30.7 %reduce-scatter.19.cloned.1.call-done = bf16[192,1536]{1,0:T(8,128)(2,1)} async-done(((bf16[768,1536]{1,0:T(8,128)(2,1)}), bf16[192,1536]{1,0:T(8,128)(2,1)}) %reduce-scatter.19.cloned.1.call-update) | async-done | bytes 589840 | tf_op jit(solution)/shard_map/reduce_scatter | solution.py:285
  559.3 35.8 %reduce-scatter.15.cloned.1.call-done = bf16[384,768]{1,0:T(8,128)(2,1)} async-done(((bf16[1536,768]{1,0:T(8,128)(2,1)}), bf16[384,768]{1,0:T(8,128)(2,1)}) %reduce-scatter.15.cloned.1.call-update) | async-done | bytes 589840 | tf_op jit(solution)/shard_map/reduce_scatter | solution.py:279
  595.1 35.2 %reduce-scatter.17.cloned.1.call-done = bf16[384,768]{1,0:T(8,128)(2,1)} async-done(((bf16[1536,768]{1,0:T(8,128)(2,1)}), bf16[384,768]{1,0:T(8,128)(2,1)}) %reduce-scatter.17.cloned.1.call-update) | async-done | bytes 589840 | tf_op jit(solution)/shard_map/reduce_scatter | solution.py:282
  630.3 99.5 %reduce-scatter.21.cloned.1.call-done = bf16[384,3968]{1,0:T(8,128)(2,1)} async-done(((bf16[1536,3968]{1,0:T(8,128)(2,1)}), bf16[384,3968]{1,0:T(8,128)(2,1)}) %reduce-scatter.21.cloned.1.call-update) | async-done | bytes 3047440 | tf_op jit(solution)/shard_map/reduce_scatter | solution.py:291
  729.8 99.5 %reduce-scatter.23.cloned.1.call-done = bf16[384,3968]{1,0:T(8,128)(2,1)} async-done(((bf16[1536,3968]{1,0:T(8,128)(2,1)}), bf16[384,3968]{1,0:T(8,128)(2,1)}) %reduce-scatter.23.cloned.1.call-update) | async-done | bytes 3047440 | tf_op jit(solution)/shard_map/reduce_scatter | solution.py:294
  835.1 39.9 %psum.67 = f32[32,12]{0,1:T(8,128)} all-reduce(f32[32,12]{0,1:T(8,128)S(1)} %copy-done.47), channel_id=1, replica_groups=mesh['group'=8,'ctx'=2,'wshard'=2] {'group','ctx','wshard'}, use_global_device_ids=true, to_apply=%region_47.49 | all-reduce | flops 384 | bytes 3072 | tf_op jit(solution)/shard_map/psum | solution.py:264
  887.7 20.0 %all-reduce.2 = (bf16[384]{0:T(512)(128)(2,1)S(1)}, bf16[384]{0:T(512)(128)(2,1)S(1)}) all-reduce(bf16[384]{0:T(512)(128)(2,1)S(1)} %dynamic-slice.2, bf16[384]{0:T(512)(128)(2,1)S(1)} %dynamic-slice.4), channel_id=1, replica_groups=mesh['group'=8,'ctx'=2,'wshard'=2] {'group'}, use_global_device_ids=true, to_apply=%region_38.40 | all-reduce | flops 768 | bytes 3072 | tf_op jit(solution)/shard_map/psum | solution.py:302
  914.6 58.3 %all-gather.39.cloned.1.call-done = bf16[3072,768]{1,0:T(8,128)(2,1)} async-done(((bf16[384,768]{1,0:T(8,128)(2,1)}), bf16[3072,768]{1,0:T(8,128)(2,1)}) %all-gather.39.cloned.1.call-update) | async-done | bytes 4718608 | tf_op jit(solution)/shard_map/all_gather | solution.py:13
  977.3 338.3 %all-reduce.7.cloned.1.call-done = (bf16[384,768]{1,0:T(8,128)(2,1)}, bf16[384,768]{1,0:T(8,128)(2,1)}, bf16[192,1536]{1,0:T(8,128)(2,1)}, bf16[384,3968]{1,0:T(...) async-done(((bf16[384,768]{1,0:T(8,128)(2,1)}, bf16[384,768]{1,0:T(8,128)(2,1)}, bf16[192,1536]{1,0:T(8,128)(2,1)}, bf16[384,3968]{1,0:T(8,128)(2,1)}, ...) | async-done | bytes 10911760 | tf_op jit(solution)/shard_map/psum | solution.py:304
  (350 shorter events, 372.0 us)
Async XLA Ops:
  7.2 16.1 %all-gather.15.cloned.1.call-start = ((), (), s32[]{:S(2)}) async-start(), calls=%async_computation.8 | async-start | bytes 3538944 | tf_op jit(solution)/shard_map/all_gather | solution.py:68
  7.9 29.0 %all-gather.19.cloned.1.call-start = ((), (), s32[]{:S(2)}) async-start(), calls=%async_computation.10 | async-start | bytes 3538944 | tf_op jit(solution)/shard_map/all_gather | solution.py:67
  8.7 42.1 %all-gather.23.cloned.1.call-start = ((), (), s32[]{:S(2)}) async-start(), calls=%async_computation.12 | async-start | bytes 3538944 | tf_op jit(solution)/shard_map/all_gather | solution.py:66
  9.4 64.2 %all-gather.17.cloned.1.call-start = ((), (), s32[]{:S(2)}) async-start(), calls=%async_computation.9 | async-start | bytes 1966080 | tf_op jit(solution)/shard_map/all_gather | solution.py:114
  9.7 41.0 %copy-start.43 = (f32[256]{0:T(256)}, f32[256]{0:T(256)S(1)}, u32[]{:S(2)}) copy-start(f32[256]{0:T(256)S(1)} %fusion.110) | copy-start | bytes 3076
  26.6 68.7 %all-gather.21.cloned.1.call-start = ((), (), s32[]{:S(2)}) async-start(), calls=%async_computation.11 | async-start | bytes 1966080 | tf_op jit(solution)/shard_map/all_gather | solution.py:113
  40.2 195.1 %all-gather.35.cloned.1.call-start = ((), (), s32[]{:S(2)}) async-start(), calls=%async_computation.18 | async-start | bytes 3932160 | tf_op jit(solution)/shard_map/all_gather | solution.py:104
  40.8 199.8 %all-gather.25.cloned.1.call-start = ((), (), s32[]{:S(2)}) async-start(), calls=%async_computation.13 | async-start | bytes 3538944 | tf_op jit(solution)/shard_map/all_gather | solution.py:69
  41.6 203.3 %all-gather.27.cloned.1.call-start = ((), (), s32[]{:S(2)}) async-start(), calls=%async_computation.14 | async-start | bytes 18284544 | tf_op jit(solution)/shard_map/all_gather | solution.py:70
  42.3 212.6 %all-gather.29.cloned.1.call-start = ((), (), s32[]{:S(2)}) async-start(), calls=%async_computation.15 | async-start | bytes 18284544 | tf_op jit(solution)/shard_map/all_gather | solution.py:71
  43.1 222.0 %all-gather.31.cloned.1.call-start = ((), (), s32[]{:S(2)}) async-start(), calls=%async_computation.16 | async-start | bytes 18284544 | tf_op jit(solution)/shard_map/all_gather | solution.py:72
  43.7 344.9 %reduce-scatter.11.cloned.1.call-start = ((), (), s32[]{:S(2)}) async-start(), calls=%async_computation.19 | async-start | bytes 3932160 | tf_op jit(solution)/shard_map/reduce_scatter | solution.py:247
  243.5 48.2 %copy-start.5 = (f32[256,1536]{1,0:T(8,128)}, f32[256,1536]{1,0:T(8,128)S(1)}, u32[]{:S(2)}) copy-start(f32[256,1536]{1,0:T(8,128)S(1)} %get-tuple-element.1287) | copy-start | bytes 4718596
  349.8 78.9 %reduce-scatter.13.cloned.1.call-start = ((), (), s32[]{:S(2)}) async-start(), calls=%async_computation.21 | async-start | bytes 2949120 | tf_op jit(solution)/shard_map/reduce_scatter | solution.py:276
  353.3 170.8 %reduce-scatter.25.cloned.1.call-start = ((), (), s32[]{:S(2)}) async-start(), calls=%async_computation.28 | async-start | bytes 15237120
  377.7 181.6 %reduce-scatter.19.cloned.1.call-start = ((), (), s32[]{:S(2)}) async-start(), calls=%async_computation.24 | async-start | bytes 2949120 | tf_op jit(solution)/shard_map/reduce_scatter | solution.py:285
  381.3 213.7 %reduce-scatter.15.cloned.1.call-start = ((), (), s32[]{:S(2)}) async-start(), calls=%async_computation.22 | async-start | bytes 2949120 | tf_op jit(solution)/shard_map/reduce_scatter | solution.py:279
  391.9 238.4 %reduce-scatter.17.cloned.1.call-start = ((), (), s32[]{:S(2)}) async-start(), calls=%async_computation.23 | async-start | bytes 2949120 | tf_op jit(solution)/shard_map/reduce_scatter | solution.py:282
  395.4 334.4 %reduce-scatter.21.cloned.1.call-start = ((), (), s32[]{:S(2)}) async-start(), calls=%async_computation.25 | async-start | bytes 15237120 | tf_op jit(solution)/shard_map/reduce_scatter | solution.py:291
  403.5 425.8 %reduce-scatter.23.cloned.1.call-start = ((), (), s32[]{:S(2)}) async-start(), calls=%async_computation.26 | async-start | bytes 15237120 | tf_op jit(solution)/shard_map/reduce_scatter | solution.py:294
  411.5 463.5 %all-gather.33.cloned.1.call-start = ((), (), s32[]{:S(2)}) async-start(), calls=%async_computation.17 | async-start | bytes 3932160 | tf_op jit(solution)/shard_map/all_gather | solution.py:266
  421.4 487.6 %all-gather.37.cloned.1.call-start = ((), (), s32[]{:S(2)}) async-start(), calls=%async_computation.20 | async-start | bytes 3932160 | tf_op jit(solution)/shard_map/all_gather | solution.py:267
  428.6 544.3 %all-gather.39.cloned.1.call-start = ((), (), s32[]{:S(2)}) async-start(), calls=%async_computation.27 | async-start | bytes 5308416 | tf_op jit(solution)/shard_map/all_gather | solution.py:13
  429.3 886.2 %all-reduce.7.cloned.1.call-start = ((), (), s32[]{:S(2)}) async-start(), calls=%async_computation.29 | async-start | bytes 21823488 | tf_op jit(solution)/shard_map/psum | solution.py:304
  (64 other events, 214.5 us)
Sparse Core Ops, SparseCore 0:
  9.5 13.6 all-gather.14
  24.8 12.1 all-gather.18
  38.5 12.1 all-gather.22
  52.7 20.8 all-gather.16
  75.6 19.6 all-gather.20
  96.6 28.4 all-gather.34
  126.7 10.9 all-gather.24
  139.3 25.4 all-gather.26
  166.3 25.5 all-gather.28
  193.3 25.4 all-gather.30
  349.9 38.6 reduce-scatter.10
  391.5 32.8 reduce-scatter.12
  427.0 96.9 reduce-scatter.24
  526.4 32.8 reduce-scatter.18
  562.3 32.7 reduce-scatter.14
  597.5 32.8 reduce-scatter.16
  632.8 97.0 reduce-scatter.20
  732.3 96.9 reduce-scatter.22
  831.5 29.0 all-gather.32
  862.5 29.1 all-gather.36
  893.8 78.9 all-gather.38
  978.7 336.7 all-reduce.6
